TPU v7x, 512 devices: a whole 4x4x16 slice. The times are simulated.
512 devices in a mesh: gx: 8 (over y, core), gy: 4 (over x), gz: 16 (over z).
Axes of the slice: x: 4, y: 4, z: 16, core: 2. Of those that a mesh axis runs over, the one named last changes fastest.
Arguments:
- level_set: float32 [128, 64, 2048], P('gx', 'gy', 'gz'), may hold values from 0 to 1
- velocity: float32 [3, 128, 64, 2048], P(None, 'gx', 'gy', 'gz'), may hold values from -6 to 6
- source: float32 [128, 64, 2048], P('gx', 'gy', 'gz'), may hold values from -6 to 6
- coarse_factor: float32 [512, 512], P(('gx', 'gy', 'gz')), may hold values from -0.2 to 0.2
Outputs:
- level_set_new: float32 [128, 64, 2048], P('gx', 'gy', 'gz')
- pressure: float32 [128, 64, 2048], P('gx', 'gy', 'gz')
All inputs are finite; a program needn't handle non-finite values.
Results may differ from a plain program's by a relative error of at most 0.029.
Values sent between devices are 32-bit elements; how exact they have to be, the bound alone decides.
A program may use at most 64 MiB of HBM per device.

v0:
```python
import jax
import jax.numpy as jnp
import numpy as np
from jax import lax
from jax.sharding import PartitionSpec as P

NP = 8
RSWEEPS = 2
ITERS = 6


GLL_POINTS = (
    -1.0,
    -0.8717401485096066,
    -0.5917001814331423,
    -0.2092992179024789,
    0.2092992179024789,
    0.5917001814331423,
    0.8717401485096066,
    1.0,
)
GLL_WEIGHTS = (
    0.03571428571428571,
    0.21070422714350603,
    0.3411226924835044,
    0.4124587946587038,
    0.4124587946587038,
    0.3411226924835044,
    0.21070422714350603,
    0.03571428571428571,
)
HIGHEST = lax.Precision.HIGHEST
TIME_STEP = 0.02
PSEUDO_STEP = 0.004
INTERFACE_WIDTH = 0.5
GAS_DENSITY = 0.1
SOURCE_SCALE = 20.0


def extended(cells, sides, width):
    for axis, dim in sides:
        count = lax.axis_size(axis)
        ends = count - 1
        head = lax.slice_in_dim(cells, 0, width, axis=dim)
        tail = lax.slice_in_dim(cells, cells.shape[dim] - width, cells.shape[dim], axis=dim)
        cells = jnp.concatenate(
            [
                lax.ppermute(tail, axis, [(i, (i + 1) % count) for i in range(ends)]),
                cells,
                lax.ppermute(head, axis, [((i + 1) % count, i) for i in range(ends)]),
            ],
            axis=dim,
        )
    return cells


def node_tables():
    points = np.array(GLL_POINTS)
    amount = points.shape[0]
    barycentric = np.ones(amount)
    for target in range(amount):
        for partner in range(amount):
            if partner != target:
                barycentric[target] = barycentric[target] / (points[target] - points[partner])
    derivative = np.zeros((amount, amount))
    for target in range(amount):
        for partner in range(amount):
            if partner != target:
                derivative[target, partner] = (
                    barycentric[partner] / barycentric[target] / (points[target] - points[partner])
                )
        derivative[target, target] = -np.sum(derivative[target])
    return derivative


def apply_axis(values, matrix, which_axis):
    if which_axis == 0:
        return jnp.einsum("ap,pqr->aqr", matrix, values, precision=HIGHEST)
    if which_axis == 1:
        return jnp.einsum("aq,pqr->par", matrix, values, precision=HIGHEST)
    return jnp.einsum("pqr,ar->pqa", values, matrix, precision=HIGHEST)


def edge_passes(padded):
    summed = padded
    for which_axis in (1, 2, 3):
        amount = summed.shape[which_axis] - 2
        center = lax.slice_in_dim(summed, 1, amount + 1, axis=which_axis)
        upper_side = lax.slice_in_dim(summed, 2, amount + 2, axis=which_axis)
        lower_side = lax.slice_in_dim(summed, 0, amount, axis=which_axis)
        shape_list = [1, 1, 1, 1]
        shape_list[which_axis] = amount
        position = (jnp.arange(amount) % NP).reshape(shape_list)
        summed = (
            center
            + jnp.where(position == NP - 1, upper_side, 0.0)
            + jnp.where(position == 0, lower_side, 0.0)
        )
    return summed


def assemble(stacked):
    padded = extended(stacked, (("gx", 1), ("gy", 2), ("gz", 3)), 1)
    return edge_passes(padded)


def body(level_set, velocity, source, coarse_factor):
    shape_tuple = level_set.shape
    derivative = node_tables()
    deriv_tables = [
        jnp.asarray(np.kron(np.eye(extent // NP), derivative), jnp.float32)
        for extent in shape_tuple
    ]
    trans_tables = [
        jnp.asarray(np.kron(np.eye(extent // NP), derivative.T), jnp.float32)
        for extent in shape_tuple
    ]
    square_tables = [
        jnp.asarray(np.kron(np.eye(extent // NP), (derivative * derivative).T), jnp.float32)
        for extent in shape_tuple
    ]
    weights = jnp.asarray(np.array(GLL_WEIGHTS), jnp.float32)
    along_x = jnp.tile(weights, shape_tuple[0] // NP)
    along_y = jnp.tile(weights, shape_tuple[1] // NP)
    along_z = jnp.tile(weights, shape_tuple[2] // NP)
    bmass = along_x[:, None, None] * along_y[None, :, None] * along_z[None, None, :]
    gradient = [
        apply_axis(level_set, deriv_tables[which_axis], which_axis) for which_axis in range(3)
    ]
    advect = velocity[0] * gradient[0] + velocity[1] * gradient[1] + velocity[2] * gradient[2]
    divergence = (
        apply_axis(bmass * velocity[0], trans_tables[0], 0)
        + apply_axis(bmass * velocity[1], trans_tables[1], 1)
        + apply_axis(bmass * velocity[2], trans_tables[2], 2)
        + bmass * source
    )
    assembled = assemble(jnp.stack([bmass * advect, bmass, divergence]))
    mass_sum = assembled[1]
    weight = bmass / mass_sum
    level_now = level_set - TIME_STEP * assembled[0] / mass_sum
    rhs_field = SOURCE_SCALE * assembled[2]
    for sweep in range(RSWEEPS):
        gradient = [
            apply_axis(level_now, deriv_tables[which_axis], which_axis) for which_axis in range(3)
        ]
        inv_norm = 1.0 / jnp.sqrt(
            1.0 + gradient[0] * gradient[0] + gradient[1] * gradient[1] + gradient[2] * gradient[2]
        )
        compress = level_now * (1.0 - level_now) * inv_norm
        weak_form = apply_axis(
            bmass * (compress * gradient[0] - INTERFACE_WIDTH * gradient[0]), trans_tables[0], 0
        )
        weak_form = weak_form + apply_axis(
            bmass * (compress * gradient[1] - INTERFACE_WIDTH * gradient[1]), trans_tables[1], 1
        )
        weak_form = weak_form + apply_axis(
            bmass * (compress * gradient[2] - INTERFACE_WIDTH * gradient[2]), trans_tables[2], 2
        )
        level_now = level_now + PSEUDO_STEP * assemble(weak_form[None])[0] / mass_sum
    inverse_density = 1.0 / (GAS_DENSITY + (1.0 - GAS_DENSITY) * jnp.clip(level_now, 0.0, 1.0))
    scaled = bmass * inverse_density
    diag_local = (
        apply_axis(scaled, square_tables[0], 0)
        + apply_axis(scaled, square_tables[1], 1)
        + apply_axis(scaled, square_tables[2], 2)
        + bmass
    )
    diagonal = assemble(diag_local[None])[0]
    own_row = coarse_factor[0]

    def precondition(residual):
        jacobi = residual / diagonal
        restricted = jnp.sum(weight * residual)
        coarse_mid = lax.psum(restricted * own_row, ("gx", "gy", "gz"))
        coarse_value = jnp.dot(own_row, coarse_mid, precision=HIGHEST)
        result = jacobi + assemble((weight * coarse_value)[None])[0]
        return (result, lax.psum(jnp.sum(weight * residual * result), ("gx", "gy", "gz")))

    pressure = jnp.zeros_like(rhs_field)
    residual = rhs_field
    direction, inner_now = precondition(residual)
    for step in range(ITERS):
        local_part = bmass * direction
        for element_which_axis in range(3):
            local_part = local_part + apply_axis(
                scaled
                * apply_axis(direction, deriv_tables[element_which_axis], element_which_axis),
                trans_tables[element_which_axis],
                element_which_axis,
            )
        image = assemble(local_part[None])[0]
        curvature = lax.psum(jnp.sum(weight * direction * image), ("gx", "gy", "gz"))
        step_size = inner_now / curvature
        pressure = pressure + step_size * direction
        residual = residual - step_size * image
        if step + 1 < ITERS:
            preconditioned, inner_next = precondition(residual)
            direction = preconditioned + inner_next / inner_now * direction
            inner_now = inner_next
    return (level_now, pressure)


def solution(mesh):
    in_specs = (
        P("gx", "gy", "gz"),
        P(None, "gx", "gy", "gz"),
        P("gx", "gy", "gz"),
        P(("gx", "gy", "gz"), None),
    )
    out_specs = (P("gx", "gy", "gz"), P("gx", "gy", "gz"))
    return jax.shard_map(body, mesh=mesh, in_specs=in_specs, out_specs=out_specs, check_vma=False)
```

profile of v0, /device:TPU:1, one launch (start us, length us, event | category | flops | bytes accessed | tf_op | source)
XLA Modules:
  0.0 2206.5 jit_solution(12459862347474892173)
XLA Ops:
  6.2 4.6 collective-permute-start
  10.8 5.5 collective-permute-start.1
  20.4 3.9 collective-permute-done.3
  37.9 4.1 collective-permute-start.6
  63.5 5.4 collective-permute-done.11
  87.6 4.9 collective-permute-start.16
  103.5 104.3 %psum.126 = f32[512]{0:T(512)S(1)} all-reduce(f32[512]{0:T(512)S(1)} %broadcast_multiply_fusion.13), channel_id=1, replica_groups=mesh['gx'=8,'gy'=4,'gz'=16] {'gx','gy','gz'}, use_global_device_ids=true, to_apply=%region_1.2 | all-reduce | flops 512 | bytes 4096 | tf_op jit(solution)/shard_map/psum | solution.py:174
  223.2 4.0 collective-permute-start.20
  240.6 4.4 collective-permute-done.23
  256.2 4.3 collective-permute-start.32
  273.4 4.8 collective-permute-done.35
  279.6 104.5 %all-reduce = (f32[]{:T(128)}, f32[]{:T(128)}) all-reduce(f32[]{:T(128)} %get-tuple-element.9, f32[]{:T(128)} %get-tuple-element.8), channel_id=1, replica_groups=mesh['gx'=8,'gy'=4,'gz'=16] {'gx','gy','gz'}, use_global_device_ids=true, to_apply=%region_3.4 | all-reduce | flops 2 | bytes 16 | tf_op jit(solution)/shard_map/psum | solution.py:177
  386.8 98.4 %psum.129 = f32[512]{0:T(512)S(1)} all-reduce(f32[512]{0:T(512)S(1)} %broadcast_multiply_fusion.12), channel_id=1, replica_groups=mesh['gx'=8,'gy'=4,'gz'=16] {'gx','gy','gz'}, use_global_device_ids=true, to_apply=%region_7.8 | all-reduce | flops 512 | bytes 4096 | tf_op jit(solution)/shard_map/psum | solution.py:174
  509.2 3.9 collective-permute-done.41
  514.5 101.3 %psum.130 = f32[]{:T(128)} all-reduce(f32[]{:T(128)} %get-tuple-element.36), channel_id=1, replica_groups=mesh['gx'=8,'gy'=4,'gz'=16] {'gx','gy','gz'}, use_global_device_ids=true, to_apply=%region_9.10 | all-reduce | flops 1 | bytes 8 | tf_op jit(solution)/shard_map/psum | solution.py:177
  645.7 102.2 %psum.131 = f32[]{:T(128)} all-reduce(f32[]{:T(128)} %get-tuple-element.34), channel_id=1, replica_groups=mesh['gx'=8,'gy'=4,'gz'=16] {'gx','gy','gz'}, use_global_device_ids=true, to_apply=%region_11.12 | all-reduce | flops 1 | bytes 8 | tf_op jit(solution)/shard_map/psum | solution.py:192
  750.5 99.1 %psum.132 = f32[512]{0:T(512)S(1)} all-reduce(f32[512]{0:T(512)S(1)} %broadcast_multiply_fusion.11), channel_id=1, replica_groups=mesh['gx'=8,'gy'=4,'gz'=16] {'gx','gy','gz'}, use_global_device_ids=true, to_apply=%region_13.14 | all-reduce | flops 512 | bytes 4096 | tf_op jit(solution)/shard_map/psum | solution.py:174
  874.0 3.9 collective-permute-done.53
  879.3 100.7 %psum.133 = f32[]{:T(128)} all-reduce(f32[]{:T(128)} %get-tuple-element.30), channel_id=1, replica_groups=mesh['gx'=8,'gy'=4,'gz'=16] {'gx','gy','gz'}, use_global_device_ids=true, to_apply=%region_15.16 | all-reduce | flops 1 | bytes 8 | tf_op jit(solution)/shard_map/psum | solution.py:177
  1009.8 102.3 %psum.134 = f32[]{:T(128)} all-reduce(f32[]{:T(128)} %get-tuple-element.28), channel_id=1, replica_groups=mesh['gx'=8,'gy'=4,'gz'=16] {'gx','gy','gz'}, use_global_device_ids=true, to_apply=%region_17.18 | all-reduce | flops 1 | bytes 8 | tf_op jit(solution)/shard_map/psum | solution.py:192
  1114.7 98.7 %psum.135 = f32[512]{0:T(512)S(1)} all-reduce(f32[512]{0:T(512)S(1)} %broadcast_multiply_fusion.10), channel_id=1, replica_groups=mesh['gx'=8,'gy'=4,'gz'=16] {'gx','gy','gz'}, use_global_device_ids=true, to_apply=%region_19.20 | all-reduce | flops 512 | bytes 4096 | tf_op jit(solution)/shard_map/psum | solution.py:174
  1237.8 3.9 collective-permute-done.65
  1243.1 100.7 %psum.136 = f32[]{:T(128)} all-reduce(f32[]{:T(128)} %get-tuple-element.24), channel_id=1, replica_groups=mesh['gx'=8,'gy'=4,'gz'=16] {'gx','gy','gz'}, use_global_device_ids=true, to_apply=%region_21.22 | all-reduce | flops 1 | bytes 8 | tf_op jit(solution)/shard_map/psum | solution.py:177
  1373.6 102.5 %psum.137 = f32[]{:T(128)} all-reduce(f32[]{:T(128)} %get-tuple-element.22), channel_id=1, replica_groups=mesh['gx'=8,'gy'=4,'gz'=16] {'gx','gy','gz'}, use_global_device_ids=true, to_apply=%region_23.24 | all-reduce | flops 1 | bytes 8 | tf_op jit(solution)/shard_map/psum | solution.py:192
  1478.7 98.7 %psum.138 = f32[512]{0:T(512)S(1)} all-reduce(f32[512]{0:T(512)S(1)} %broadcast_multiply_fusion.9), channel_id=1, replica_groups=mesh['gx'=8,'gy'=4,'gz'=16] {'gx','gy','gz'}, use_global_device_ids=true, to_apply=%region_25.26 | all-reduce | flops 512 | bytes 4096 | tf_op jit(solution)/shard_map/psum | solution.py:174
  1601.8 3.9 collective-permute-done.77
  1607.0 100.7 %psum.139 = f32[]{:T(128)} all-reduce(f32[]{:T(128)} %get-tuple-element.18), channel_id=1, replica_groups=mesh['gx'=8,'gy'=4,'gz'=16] {'gx','gy','gz'}, use_global_device_ids=true, to_apply=%region_27.28 | all-reduce | flops 1 | bytes 8 | tf_op jit(solution)/shard_map/psum | solution.py:177
  1737.5 102.3 %psum.140 = f32[]{:T(128)} all-reduce(f32[]{:T(128)} %get-tuple-element.16), channel_id=1, replica_groups=mesh['gx'=8,'gy'=4,'gz'=16] {'gx','gy','gz'}, use_global_device_ids=true, to_apply=%region_29.30 | all-reduce | flops 1 | bytes 8 | tf_op jit(solution)/shard_map/psum | solution.py:192
  1842.5 98.7 %psum.141 = f32[512]{0:T(512)S(1)} all-reduce(f32[512]{0:T(512)S(1)} %broadcast_multiply_fusion.8), channel_id=1, replica_groups=mesh['gx'=8,'gy'=4,'gz'=16] {'gx','gy','gz'}, use_global_device_ids=true, to_apply=%region_31.32 | all-reduce | flops 512 | bytes 4096 | tf_op jit(solution)/shard_map/psum | solution.py:174
  1965.6 3.9 collective-permute-done.89
  1970.8 100.7 %psum.142 = f32[]{:T(128)} all-reduce(f32[]{:T(128)} %get-tuple-element.12), channel_id=1, replica_groups=mesh['gx'=8,'gy'=4,'gz'=16] {'gx','gy','gz'}, use_global_device_ids=true, to_apply=%region_33.34 | all-reduce | flops 1 | bytes 8 | tf_op jit(solution)/shard_map/psum | solution.py:177
  2102.2 102.1 %psum.143 = f32[]{:T(128)} all-reduce(f32[]{:T(128)} %fusion.92), channel_id=1, replica_groups=mesh['gx'=8,'gy'=4,'gz'=16] {'gx','gy','gz'}, use_global_device_ids=true, to_apply=%region_35.36 | all-reduce | flops 1 | bytes 8 | tf_op jit(solution)/shard_map/psum | solution.py:192
  (429 shorter events, 405.3 us)
Async XLA Ops:
  6.2 10.1 collective-permute-start
  54.7 8.8 collective-permute-start.10
  58.3 10.6 collective-permute-start.11
  87.6 10.1 collective-permute-start.16
  92.5 9.1 collective-permute-start.17
  209.1 10.4 collective-permute-start.24
  211.1 8.4 collective-permute-start.25
  214.4 8.8 collective-permute-start.18
  219.6 9.2 collective-permute-start.26
  223.2 8.3 collective-permute-start.20
  228.9 8.1 collective-permute-start.28
  230.2 8.5 collective-permute-start.29
  231.8 8.8 collective-permute-start.22
  235.7 9.3 collective-permute-start.23
  265.1 8.3 collective-permute-start.34
  268.2 10.0 collective-permute-start.35
  500.5 8.7 collective-permute-start.40
  504.2 8.9 collective-permute-start.41
  632.6 7.9 collective-permute-start.46
  635.3 9.1 collective-permute-start.47
  865.3 8.7 collective-permute-start.52
  869.0 8.9 collective-permute-start.53
  999.4 9.1 collective-permute-start.59
  1229.1 8.7 collective-permute-start.64
  1232.8 8.9 collective-permute-start.65
  1363.2 9.1 collective-permute-start.71
  1593.1 8.7 collective-permute-start.76
  1596.8 8.9 collective-permute-start.77
  1727.1 9.1 collective-permute-start.83
  1956.9 8.7 collective-permute-start.88
  1960.6 8.9 collective-permute-start.89
  2091.0 9.1 collective-permute-start.95
  (73 other events, 550.5 us)
where the time goes:
time: 2220 us; the launch traced here: 2210 us
  blocking collectives  1720 us (77%)
  starting transfers between devices  211 us (10%)
  waiting for transfers between devices  199 us (9%)
  other arithmetic  36.4 us (2%)
    psum x6, blocking collectives, precondition(): lax.psum(jnp.sum(weight * residual * result), ('gx', 'gy', 'gz'))  609 us
    psum x6, blocking collectives, precondition(): coarse_mid = lax.psum(restricted * own_row, ('gx', 'gy', 'gz'))  598 us
    psum x5, blocking collectives, body(): lax.psum(jnp.sum(weight * direction * image), ('gx', 'gy', 'gz'))  511 us
    ppermute x48, waiting for transfers between devices, extended(): lax.ppermute(head, axis, [((i + 1) % count, i) for i in range(ends)])  147 us
    ppermute x48, starting transfers between devices, extended(): lax.ppermute(tail, axis, [(i, (i + 1) % count) for i in range(ends)])  133 us
    ppermute x48, starting transfers between devices, extended(): lax.ppermute(head, axis, [((i + 1) % count, i) for i in range(ends)])  77.4 us
    ppermute x48, waiting for transfers between devices, extended(): lax.ppermute(tail, axis, [(i, (i + 1) % count) for i in range(ends)])  51.5 us
  transfers between devices with their start and end apart: 96, of which 59 were waited for; matrix products, arithmetic and copies ran while one was open for 0% of the time, Pallas kernels for 0%

commit v1 on v0

v1 whole, which is shorter than its diff:
```python
import functools

import jax
import jax.numpy as jnp
import numpy as np
from jax import lax
from jax.experimental import pallas as pl
from jax.experimental.pallas import tpu as pltpu
from jax.sharding import PartitionSpec as P

NP = 8
RSWEEPS = 2
ITERS = 6

GLL_POINTS = (
    -1.0,
    -0.8717401485096066,
    -0.5917001814331423,
    -0.2092992179024789,
    0.2092992179024789,
    0.5917001814331423,
    0.8717401485096066,
    1.0,
)
GLL_WEIGHTS = (
    0.03571428571428571,
    0.21070422714350603,
    0.3411226924835044,
    0.4124587946587038,
    0.4124587946587038,
    0.3411226924835044,
    0.21070422714350603,
    0.03571428571428571,
)
HIGHEST = lax.Precision.HIGHEST
TIME_STEP = 0.02
PSEUDO_STEP = 0.004
INTERFACE_WIDTH = 0.5
GAS_DENSITY = 0.1
SOURCE_SCALE = 20.0
MESH = pl.DeviceIdType.MESH
AXES = ("gx", "gy", "gz")
LANES = 128
OFFSETS = tuple(
    (i, j, k) for i in (-1, 0, 1) for j in (-1, 0, 1) for k in (-1, 0, 1) if (i, j, k) != (0, 0, 0)
)


def node_tables():
    points = np.array(GLL_POINTS)
    amount = points.shape[0]
    barycentric = np.ones(amount)
    for target in range(amount):
        for partner in range(amount):
            if partner != target:
                barycentric[target] = barycentric[target] / (points[target] - points[partner])
    derivative = np.zeros((amount, amount))
    for target in range(amount):
        for partner in range(amount):
            if partner != target:
                derivative[target, partner] = (
                    barycentric[partner] / barycentric[target] / (points[target] - points[partner])
                )
        derivative[target, target] = -np.sum(derivative[target])
    return derivative


def two_parts(matrix):
    matrix = matrix.astype(np.float32)
    high = matrix.astype(jnp.bfloat16)
    low = (matrix - high.astype(np.float32)).astype(jnp.bfloat16)
    return high, low


def block_tables(nx, ny, nz):
    d = node_tables()
    sq = (d * d).T

    def blocks(n, m):
        return np.kron(np.eye(n // NP), m)

    along_x = np.kron(blocks(nx, d), np.eye(ny))
    along_y = np.kron(np.eye(nx), blocks(ny, d))
    left = np.concatenate([along_x, along_y], axis=0)
    square = np.kron(blocks(nx, sq), np.eye(ny)) + np.kron(np.eye(nx), blocks(ny, sq))
    w = np.array(GLL_WEIGHTS, np.float32)
    rows = (np.tile(w, nx // NP)[:, None] * np.tile(w, ny // NP)[None, :]).reshape(-1, 1)
    mass = (rows * np.tile(w, nz // NP)[None, :]).astype(np.float32)
    tables = []
    for m in (left, left.T, blocks(nz, d.T), blocks(nz, d), square, blocks(nz, d * d)):
        tables.extend(two_parts(m))
    return tables, mass


def parts_of(value):
    high = value.astype(jnp.bfloat16)
    low = (value - high.astype(jnp.float32)).astype(jnp.bfloat16)
    return high, low


def mm(a, b):
    return jnp.dot(a, b, preferred_element_type=jnp.float32)


def left_product(high, low, parts):
    return mm(high, parts[0]) + (mm(high, parts[1]) + mm(low, parts[0]))


def right_product(parts, high, low):
    return mm(parts[0], high) + (mm(parts[1], high) + mm(parts[0], low))


def exact(a, b, ca, cb):
    return lax.dot_general(
        a, b, (((ca,), (cb,)), ((), ())), precision=HIGHEST, preferred_element_type=jnp.float32
    )


def kernel(cfg, *refs):
    sizes, nx, ny, nz, ncoarse = cfg
    sx, sy, sz = sizes
    rows = nx * ny
    crows = ncoarse // LANES
    halves = rows // LANES
    (ls, vel, src, xrow) = refs[:4]
    (lxh, lxl, lth, ltl, rzh, rzl, rth, rtl, sqh, sql, szh, szl) = refs[4:16]
    mass = refs[16]
    lev_out, p_out = refs[17:19]
    (
        qs, ysend, zsend, recvf, recvz, az, msg, arp, arz, xnb, xin, zmask, phi, wt, ibw, scaled, invd,
        rf, zf, pf, apf, mv, ends, sxy, rxy, rzs, ssa, rpa, rza, xss, xrs,
    ) = refs[19:]

    me = [lax.axis_index(a) for a in AXES]

    def device(offset):
        return tuple(
            lax.rem(me[i] + (offset[i] % sizes[i]), sizes[i]) if offset[i] % sizes[i] else me[i]
            for i in range(3)
        )

    plane_peers = [(i, j, 0) for i in range(sx) for j in range(sy) if (i, j) != (0, 0)]
    line_peers = [(0, 0, k) for k in range(1, sz)]

    has_lo = [jnp.where(me[i] > 0, 1.0, 0.0).astype(jnp.float32) for i in range(3)]
    has_hi = [jnp.where(me[i] < sizes[i] - 1, 1.0, 0.0).astype(jnp.float32) for i in range(3)]

    row = lax.broadcasted_iota(jnp.int32, (rows, 1), 0)
    lane = lax.broadcasted_iota(jnp.int32, (1, nz), 1)
    row_x, row_y = lax.shift_right_logical(row, ny.bit_length() - 1), lax.bitwise_and(row, ny - 1)

    def inverse_copies(index, extent, dim):
        inside = lax.bitwise_and(index, NP - 1)
        low = (inside == 0) & (index > 0)
        high = (inside == NP - 1) & (index < extent - 1)
        value = jnp.where(low | high, 0.5, 1.0).astype(jnp.float32)
        value = value - jnp.where(index == 0, 0.5, 0.0) * has_lo[dim]
        return value - jnp.where(index == extent - 1, 0.5, 0.0) * has_hi[dim]

    weight = inverse_copies(row_x, nx, 0) * inverse_copies(row_y, ny, 1) * inverse_copies(lane, nz, 2)
    wt[...] = weight
    ibw[...] = weight / mass[...]

    def spread_shape(index, extent, dim, which):
        at_low = jnp.where(index == 0, 0.5, 0.0) * has_lo[dim]
        at_high = jnp.where(index == extent - 1, 0.5, 0.0) * has_hi[dim]
        own = 1.0 - at_low - at_high
        return jnp.where(which == 0, at_low, jnp.where(which == 1, own, at_high))

    flat = lax.broadcasted_iota(jnp.int32, (1, rows), 1)
    flat_x = lax.shift_right_logical(flat, ny.bit_length() - 1)
    flat_y = lax.bitwise_and(flat, ny - 1)

    def split_nine(count):
        k = lax.broadcasted_iota(jnp.int32, (count, 1), 0)
        first = jnp.where(k >= 3, 1, 0) + jnp.where(k >= 6, 1, 0)
        return k, first, k - 3 * first

    k9, kx, ky = split_nine(16)
    both = spread_shape(flat_x, nx, 0, kx) * spread_shape(flat_y, ny, 1, ky)
    phi[...] = jnp.where(k9 < 9, both, 0.0)
    phi_z = [spread_shape(lane, nz, 2, jnp.full((1, nz), kz, jnp.int32)) for kz in range(3)]

    k18 = lax.broadcasted_iota(jnp.int32, (18, 1), 0)
    upper = jnp.where(k18 >= 9, 1, 0)
    k_in = k18 - 9 * upper
    zx = jnp.where(k_in >= 3, 1, 0) + jnp.where(k_in >= 6, 1, 0)
    zy = k_in - 3 * zx

    def region(index, extent, dim, which):
        at_low = jnp.where(index == 0, 1.0, 0.0) * has_lo[dim]
        at_high = jnp.where(index == extent - 1, 1.0, 0.0) * has_hi[dim]
        return jnp.where(which == 0, at_low, jnp.where(which == 1, 1.0, at_high))

    side = jnp.where(upper == 0, has_lo[2], has_hi[2])
    zmask[...] = region(flat_x, nx, 0, zx) * region(flat_y, ny, 1, zy) * side
    wide_lane = lax.broadcasted_iota(jnp.int32, (18, nz), 1)
    target = jnp.where(k18 < 9, 0, nz - 1)
    ends[...] = jnp.where(wide_lane == target, 1.0, 0.0)
    pick_row = lax.broadcasted_iota(jnp.int32, (8, nz), 0)
    pick_lane = lax.broadcasted_iota(jnp.int32, (8, nz), 1)
    pick = jnp.where(
        ((pick_row == 0) & (pick_lane == 0)) | ((pick_row == 1) & (pick_lane == nz - 1)), 1.0, 0.0
    )

    xnb[...] = jnp.zeros_like(xnb)
    for j in range(crows):
        xnb[1, 4:5, j * LANES : (j + 1) * LANES] = xrow[j : j + 1, :]
    for par in range(2):
        msg[par] = jnp.zeros_like(msg[par])
    pf[...] = jnp.zeros_like(pf)
    apf[...] = jnp.zeros_like(apf)
    mv[...] = jnp.zeros_like(mv)
    p_out[...] = jnp.zeros_like(p_out)

    barrier = pltpu.get_barrier_semaphore()
    peers = sorted(
        {tuple(o[i] % sizes[i] for i in range(3)) for o in OFFSETS}
        | set(plane_peers)
        | set(line_peers)
    )
    for o in peers:
        pl.semaphore_signal(barrier, inc=1, device_id=device(o), device_id_type=MESH)
    pl.semaphore_wait(barrier, len(peers))

    def remote(source, dest, send, recv, offset):
        return pltpu.make_async_remote_copy(
            src_ref=source,
            dst_ref=dest,
            send_sem=send,
            recv_sem=recv,
            device_id=device(offset),
            device_id_type=MESH,
        )

    def drain(ref, sem):
        pltpu.make_async_copy(ref, ref, sem).wait()

    def nine(o):
        return (1 - o[0]) * 3 + (1 - o[1])

    for o in OFFSETS:
        place = pl.ds(OFFSETS.index(o) * crows, crows)
        remote(xrow, xin.at[place, :], xss.at[0], xrs.at[0], o).start()

    face_rows = 2 * ny + 2 * nx

    def halo_start(value, slot):
        inside = lax.bitwise_and(lane, NP - 1)
        up = (inside == NP - 1) & (lane < nz - 1)
        down = (inside == 0) & (lane > 0)
        q = (
            value
            + jnp.where(up, pltpu.roll(value, nz - 1, 1), 0.0)
            + jnp.where(down, pltpu.roll(value, 1, 1), 0.0)
        )
        field = qs.at[slot]
        field[...] = q
        for e in range(NP, ny, NP):
            total = field[pl.ds(e - 1, nx, stride=ny), :] + field[pl.ds(e, nx, stride=ny), :]
            field[pl.ds(e - 1, nx, stride=ny), :] = total
            field[pl.ds(e, nx, stride=ny), :] = total
        for e in range(NP, nx, NP):
            total = field[(e - 1) * ny : e * ny, :] + field[e * ny : (e + 1) * ny, :]
            field[(e - 1) * ny : e * ny, :] = total
            field[e * ny : (e + 1) * ny, :] = total
        ysend[slot, 0] = field[pl.ds(0, nx, stride=ny), :]
        ysend[slot, 1] = field[pl.ds(ny - 1, nx, stride=ny), :]
        face = exact(pick, field[...], 1, 1)
        for dx in (-1, 0, 1):
            for dy in (-1, 0, 1):
                shift = (-ny * dx + (ny - 1) * dy) % rows
                moved = pltpu.roll(face, shift, 1) if shift else face
                place = (dx + 1) * 3 + dy + 1
                for h in range(halves):
                    part = moved[0:2, h * LANES : (h + 1) * LANES]
                    zsend[slot, place, h : h + 1, :] = part[0:1]
                    zsend[slot, place, halves + h : halves + h + 1, :] = part[1:2]
        send, recv = sxy.at[slot], rxy.at[slot]
        for o in OFFSETS:
            if o[2] != 0:
                k, hi = nine(o), 1 if o[2] > 0 else 0
                remote(
                    zsend.at[slot, k, pl.ds(hi * halves, halves), :],
                    recvz.at[slot, pl.ds((k + (0 if hi else 9)) * halves, halves), :],
                    rzs.at[slot, 0],
                    rzs.at[slot, 1],
                    o,
                ).start()
        for o in OFFSETS:
            if o[2] == 0:
                x_row = 0 if o[0] < 0 else (nx - 1) * ny
                y_row = 0 if o[1] < 0 else ny - 1
                if o[1] == 0:
                    source = qs.at[slot, pl.ds(x_row, ny), :]
                    place, count = (0 if o[0] > 0 else ny), ny
                elif o[0] == 0:
                    source = ysend.at[slot, 0 if o[1] < 0 else 1]
                    place, count = 2 * ny + (0 if o[1] > 0 else nx), nx
                else:
                    source = qs.at[slot, pl.ds(x_row + y_row, 1), :]
                    place = face_rows + (0 if o[0] > 0 else 2) + (0 if o[1] > 0 else 1)
                    count = 1
                remote(source, recvf.at[slot, pl.ds(place, count), :], send, recv, o).start()

    def halo_finish(slot):
        drain(recvf.at[slot], rxy.at[slot])
        drain(recvz.at[slot], rzs.at[slot, 1])
        for h in range(halves):
            piece = slice(h * LANES, (h + 1) * LANES)
            arrived = recvz[slot, pl.ds(h, 18, stride=halves), :] * zmask[:, piece]
            az[piece, :] = qs[slot, piece, :] + exact(arrived, ends[...], 0, 0)
        faces = recvf.at[slot]
        az[0:ny, :] += faces[0:ny, :] * has_lo[0]
        az[rows - ny : rows, :] += faces[ny : 2 * ny, :] * has_hi[0]
        az[pl.ds(0, nx, stride=ny), :] += faces[2 * ny : 2 * ny + nx, :] * has_lo[1]
        az[pl.ds(ny - 1, nx, stride=ny), :] += faces[2 * ny + nx : face_rows, :] * has_hi[1]
        corners = (
            (0, has_lo[0] * has_lo[1]),
            (ny - 1, has_lo[0] * has_hi[1]),
            (rows - ny, has_hi[0] * has_lo[1]),
            (rows - 1, has_hi[0] * has_hi[1]),
        )
        for n, (place, flag) in enumerate(corners):
            az[place : place + 1, :] += faces[face_rows + n : face_rows + n + 1, :] * flag
        drain(recvf.at[slot], sxy.at[slot])
        drain(recvz.at[slot], rzs.at[slot, 0])
        return az[...]

    mrows = crows + 1

    def plane_start(par):
        for n, o in enumerate(plane_peers):
            remote(
                msg.at[par, 0, pl.ds(0, mrows), :], arp.at[par, n], ssa.at[par, 0], rpa.at[par], o
            ).start()

    def plane_finish_line_start(par):
        drain(arp.at[par], rpa.at[par])
        msg[par, 1, 0:mrows] = msg[par, 0, 0:mrows] + jnp.sum(arp[par], axis=0)
        for n, o in enumerate(line_peers):
            remote(
                msg.at[par, 1, pl.ds(0, mrows), :], arz.at[par, n], ssa.at[par, 1], rza.at[par], o
            ).start()

    def line_finish(par):
        drain(arz.at[par], rza.at[par])
        total = msg[par, 1, 0:mrows] + jnp.sum(arz[par], axis=0)
        drain(arp.at[par], ssa.at[par, 0])
        drain(arz.at[par], ssa.at[par, 1])
        return total

    def grad(value):
        parts = parts_of(value)
        gxy = left_product(lxh[...], lxl[...], parts)
        return gxy, right_product(parts, rzh[...], rzl[...])

    def grad_transposed(wxy, wz):
        return left_product(lth[...], ltl[...], parts_of(wxy)) + right_product(
            parts_of(wz), rth[...], rtl[...]
        )

    def twice(value):
        return jnp.concatenate([value, value], axis=0)

    def total_of(value):
        return jnp.sum(jnp.sum(value, axis=0, keepdims=True), axis=1, keepdims=True)

    def spread(coarse):
        acc = jnp.zeros((16, nz), jnp.float32)
        for kz in range(3):
            product = xnb[kz, :, 0:LANES] * coarse[0:1, :]
            for j in range(1, crows):
                product = product + xnb[kz, :, j * LANES : (j + 1) * LANES] * coarse[j : j + 1, :]
            acc = acc + jnp.sum(product, axis=1, keepdims=True) * phi_z[kz]
        return exact(phi[...], acc, 0, 0)

    level = ls[...]
    gxy, gz = grad(level)
    advect = vel[0] * gxy[0:rows] + vel[1] * gxy[rows:] + vel[2] * gz
    b = mass[...]
    halo_start(b * advect, 0)
    halo_start(
        grad_transposed(jnp.concatenate([b * vel[0], b * vel[1]], axis=0), b * vel[2])
        + b * src[...],
        1,
    )
    level = level - TIME_STEP * halo_finish(0) * ibw[...]
    rhs = SOURCE_SCALE * halo_finish(1)
    rf[...] = rhs
    restricted = total_of(wt[...] * rhs)
    for j in range(crows):
        msg[1, 0, j : j + 1, :] = restricted * xrow[j : j + 1, :]
    plane_start(1)
    for sweep in range(RSWEEPS):
        gxy, gz = grad(level)
        gx, gy = gxy[0:rows], gxy[rows:]
        inv_norm = lax.rsqrt(1.0 + gx * gx + gy * gy + gz * gz)
        factor = mass[...] * (level * (1.0 - level) * inv_norm - INTERFACE_WIDTH)
        slot = (2 + sweep) % 3
        halo_start(grad_transposed(twice(factor) * gxy, factor * gz), slot)
        if sweep == 0:
            plane_finish_line_start(1)
        level = level + PSEUDO_STEP * halo_finish(slot) * ibw[...]
    lev_out[...] = level

    b = mass[...]
    sc = b / (GAS_DENSITY + (1.0 - GAS_DENSITY) * jnp.clip(level, 0.0, 1.0))
    scaled[...] = sc
    parts = parts_of(sc)
    halo_start(
        left_product(sqh[...], sql[...], parts) + right_product(parts, szh[...], szl[...]) + b, 1
    )
    coarse = line_finish(1)
    mv[0, 0:crows] = coarse[0:crows]
    drain(xin, xrs.at[0])
    drain(xin, xss.at[0])
    for n, o in enumerate(OFFSETS):
        for j in range(crows):
            xnb[1 - o[2], nine(o) : nine(o) + 1, j * LANES : (j + 1) * LANES] = xin[
                n * crows + j : n * crows + j + 1, :
            ]
    spread_now = spread(coarse)
    inverse = 1.0 / halo_finish(1)
    invd[...] = inverse
    zf[...] = rf[...] * inverse + spread_now

    def element_operator(value):
        gxy, gz = grad(value)
        sc = scaled[...]
        return grad_transposed(twice(sc) * gxy, sc * gz) + mass[...] * value

    lane1 = lax.broadcasted_iota(jnp.int32, (1, LANES), 1)

    def send_sums(par, z, q):
        inner = total_of(wt[...] * rf[...] * z)
        energy = total_of(q * z)
        cross = total_of(q * pf[...])
        msg[par, 0, crows : crows + 1, :] = jnp.where(
            lane1 == 0, inner, jnp.where(lane1 == 1, energy, jnp.where(lane1 == 2, cross, 0.0))
        )

    def steps_from(total, step):
        sums = total[crows : crows + 1, :]
        inner, energy, cross = sums[:, 0:1], sums[:, 1:2], sums[:, 2:3]
        old_inner, old_curve = mv[2, 0:1, 0:1], mv[2, 1:2, 0:1]
        ratio = jnp.where(step > 0, inner / old_inner, 0.0)
        curve = energy + 2.0 * ratio * cross + ratio * ratio * old_curve
        return inner, ratio, curve, inner / curve

    mv[2] = jnp.ones((8, LANES), jnp.float32)

    def iteration(step, carry):
        slot = lax.rem(step, 2)
        z = zf[...]
        q = element_operator(z)
        tested = exact(phi[...], q, 1, 0)
        columns = [jnp.sum(tested * phi_z[kz], axis=1, keepdims=True) for kz in range(3)]
        for j in range(crows):
            part = columns[0] * xnb[0, :, j * LANES : (j + 1) * LANES]
            for kz in (1, 2):
                part = part + columns[kz] * xnb[kz, :, j * LANES : (j + 1) * LANES]
            msg[slot, 0, j : j + 1, :] = jnp.sum(part, axis=0, keepdims=True)
        send_sums(slot, z, q)
        plane_start(slot)
        halo_start(q, slot)
        plane_finish_line_start(slot)
        az_now = halo_finish(slot)
        total = line_finish(slot)
        inner, ratio, curve, size = steps_from(total, step)
        p = z + ratio * pf[...]
        ap = az_now + ratio * apf[...]
        pf[...] = p
        apf[...] = ap
        p_out[...] += size * p
        r = rf[...] - size * ap
        rf[...] = r
        mv[1, 0:crows] = total[0:crows] + ratio * mv[1, 0:crows]
        coarse = mv[0, 0:crows] - size * mv[1, 0:crows]
        mv[0, 0:crows] = coarse
        mv[2, 0:1, :] = jnp.broadcast_to(inner, (1, LANES))
        mv[2, 1:2, :] = jnp.broadcast_to(curve, (1, LANES))
        zf[...] = r * invd[...] + spread(coarse)
        return carry

    lax.fori_loop(0, ITERS - 1, iteration, 0)

    par = (ITERS - 1) % 2
    z = zf[...]
    send_sums(par, z, element_operator(z))
    plane_start(par)
    plane_finish_line_start(par)
    _, ratio, _, size = steps_from(line_finish(par), ITERS - 1)
    p_out[...] += size * (z + ratio * pf[...])


def body(sizes, level_set, velocity, source, coarse_factor):
    nx, ny, nz = level_set.shape
    rows = nx * ny
    ncoarse = coarse_factor.shape[1]
    crows = ncoarse // LANES
    tables, mass = block_tables(nx, ny, nz)
    sx, sy, sz = sizes
    f32 = jnp.float32

    def vm(*shape):
        return pltpu.VMEM(shape, f32)

    dma = pltpu.SemaphoreType.DMA
    face_rows = 2 * ny + 2 * nx
    halves = rows // LANES
    scratch = [
        vm(3, rows, nz),
        vm(3, 2, nx, nz),
        vm(3, 9, 2 * halves, LANES),
        vm(3, face_rows + 4, nz),
        vm(3, 18 * halves, LANES),
        vm(rows, nz),
        vm(2, 2, 8, LANES),
        vm(2, sx * sy - 1, crows + 1, LANES),
        vm(2, sz - 1, crows + 1, LANES),
        vm(3, 16, ncoarse),
        vm(len(OFFSETS) * crows, LANES),
        vm(18, rows),
        vm(16, rows),
        vm(rows, nz),
        vm(rows, nz),
        vm(rows, nz),
        vm(rows, nz),
        vm(rows, nz),
        vm(rows, nz),
        vm(rows, nz),
        vm(rows, nz),
        vm(3, 8, LANES),
        vm(18, nz),
        dma((3,)),
        dma((3,)),
        dma((3, 2)),
        dma((2, 2)),
        dma((2,)),
        dma((2,)),
        dma((1,)),
        dma((1,)),
    ]
    flat = level_set.reshape(rows, nz)
    level, pressure = pl.pallas_call(
        functools.partial(kernel, (sizes, nx, ny, nz, ncoarse)),
        out_shape=(jax.ShapeDtypeStruct((rows, nz), f32),) * 2,
        in_specs=[pl.BlockSpec(memory_space=pltpu.VMEM)] * (5 + len(tables)),
        out_specs=(pl.BlockSpec(memory_space=pltpu.VMEM),) * 2,
        scratch_shapes=scratch,
        compiler_params=pltpu.CompilerParams(
            collective_id=0, has_side_effects=True, vmem_limit_bytes=48 * 1024 * 1024
        ),
        name="transport_and_pressure",
    )(
        flat,
        velocity.reshape(3, rows, nz),
        source.reshape(rows, nz),
        coarse_factor.reshape(crows, LANES),
        *[jnp.asarray(t) for t in tables],
        jnp.asarray(mass),
    )
    return level.reshape(nx, ny, nz), pressure.reshape(nx, ny, nz)


def solution(mesh):
    sizes = tuple(mesh.shape[a] for a in AXES)
    in_specs = (
        P("gx", "gy", "gz"),
        P(None, "gx", "gy", "gz"),
        P("gx", "gy", "gz"),
        P(("gx", "gy", "gz"), None),
    )
    out_specs = (P("gx", "gy", "gz"), P("gx", "gy", "gz"))
    return jax.shard_map(
        functools.partial(body, sizes),
        mesh=mesh,
        in_specs=in_specs,
        out_specs=out_specs,
        check_vma=False,
    )
```

time: 2220 us -> 148 us (0.07)
  blocking collectives: 1720 us -> 0 us
  starting transfers between devices: 211 us -> 0 us
  waiting for transfers between devices: 199 us -> 0 us
  Pallas kernels: 0 us -> 131 us
  other arithmetic: 36.4 us -> 0 us
    psum x17 -> x0, blocking collectives: 1720 us -> none  [the longest x6 609 us: precondition(): lax.psum(jnp.sum(weight * residual * result), ('gx', 'gy', 'gz'))]
    ppermute x96 -> x0, starting transfers between devices: 211 us -> none  [the longest x48 133 us: extended(): lax.ppermute(tail, axis, [(i, (i + 1) % count) for i in range(ends)])]
    ppermute x96 -> x0, waiting for transfers between devices: 199 us -> none  [the longest x48 147 us: extended(): lax.ppermute(head, axis, [((i + 1) % count, i) for i in range(ends)])]
    pallas_call x0 -> x1, Pallas kernels: none -> 131 us  [body(): pl.pallas_call(functools.partial(kernel, (sizes, nx, ny, nz, ncoarse)), o...]
  transfers between devices with their start and end apart: 96 -> 0, of which waited for: 59 -> 0; matrix products, arithmetic and copies ran while one was open for 0% -> 0% of each run, Pallas kernels for 0% -> 0%
where the time goes in v1:
time: 148 us; the launch traced here: 147 us
  Pallas kernels  131 us (89%)
  local copies, waits for them, and re-layouts  15.8 us (11%)
    pallas_call x1, Pallas kernels, body(): pl.pallas_call(functools.partial(kernel, (sizes, nx, ny, nz, ncoarse)), o...  131 us
    unnamed x36, local copies, waits for them, and re-layouts  15.8 us

profile of v1, /device:TPU:1, one launch (start us, length us, event | category | flops | bytes accessed | tf_op | source)
XLA Modules:
  0.0 147.3 jit_solution(7910440084147729288)
XLA Ops:
  0.6 0.0 copy-start.16
  0.6 0.7 copy-done.16
  1.3 0.0 copy-start
  1.3 1.0 copy-done
  2.3 0.0 copy-start.1
  2.3 0.9 copy-done.1
  3.3 0.0 copy-start.2
  3.3 0.9 copy-done.2
  4.2 0.0 copy-start.3
  4.2 0.9 copy-done.3
  5.2 0.0 copy-start.4
  5.2 0.9 copy-done.4
  6.1 0.0 copy-start.5
  6.1 0.9 copy-done.5
  7.0 0.0 copy-start.6
  7.0 0.9 copy-done.6
  7.9 0.0 copy-start.7
  7.9 0.9 copy-done.7
  8.8 0.0 copy-start.8
  8.8 0.9 copy-done.8
  9.7 0.0 copy-start.9
  9.7 0.9 copy-done.9
  10.6 0.0 copy-start.10
  10.6 0.8 copy-done.10
  11.4 0.8 copy-done.11
  12.2 0.8 copy-done.12
  12.9 0.8 copy-done.13
  13.7 0.8 copy-done.14
  14.4 0.8 copy-done.15
  15.2 130.8 %transport_and_pressure.1 = (f32[256,128]{1,0:T(8,128)S(1)}, f32[256,128]{1,0:T(8,128)S(1)}) custom-call(f32[256,128]{1,0:T(8,128)S(1)} %bitcast.9, f32[3,256,128]{2,1,0:T(8,128)S(1)} %bitcast.6, f32[256,128]{1,0:T(8,128)S(1)} %bitcast.10, f32[4,128]{1,0:T(4,128)S(1)} %bitcast.11, bf16[512,256]{1,0:T(8,128)(2,1)S(1)} %copy-done.4, ...), custom_call_target="tpu_custom_call" | custom-call | tf_op jit(solution)/shard_map/transport_and_pressure/pallas_call | solution.py:546
  146.0 0.7 copy.21
  146.7 0.7 copy.22
  (5 shorter events, 0.0 us)
Async XLA Ops:
  0.6 0.7 copy-start.16
  1.3 1.0 copy-start
  2.3 0.9 copy-start.1
  3.3 0.9 copy-start.2
  4.2 0.9 copy-start.3
  5.2 0.9 copy-start.4
  6.1 0.9 copy-start.5
  7.0 0.9 copy-start.6
  7.9 0.9 copy-start.7
  8.8 0.9 copy-start.8
  9.7 0.9 copy-start.9
  10.6 0.8 copy-start.10
  11.4 0.8 copy-start.11
  12.2 0.8 copy-start.12
  12.9 0.8 copy-start.13
  13.7 0.8 copy-start.14
  14.4 0.8 copy-start.15

commit v2 on v1

--- a/solution.py
+++ b/solution.py
@@ -87,9 +87,14 @@
     rows = (np.tile(w, nx // NP)[:, None] * np.tile(w, ny // NP)[None, :]).reshape(-1, 1)
     mass = (rows * np.tile(w, nz // NP)[None, :]).astype(np.float32)
     tables = []
-    for m in (left, left.T, blocks(nz, d.T), blocks(nz, d), square, blocks(nz, d * d)):
+    for m in (left, left.T):
         tables.extend(two_parts(m))
-    return tables, mass
+    for m in (blocks(nz, d.T), blocks(nz, d)):
+        high, low = two_parts(m)
+        tables.extend((np.concatenate([high, low], axis=1), high))
+    tables.append(np.stack(two_parts(square)))
+    tables.append(np.concatenate(two_parts(blocks(nz, d * d)), axis=1))
+    return tables + [mass]
 
 
 def parts_of(value):
@@ -102,12 +107,18 @@
     return jnp.dot(a, b, preferred_element_type=jnp.float32)
 
 
-def left_product(high, low, parts):
-    return mm(high, parts[0]) + (mm(high, parts[1]) + mm(low, parts[0]))
-
-
-def right_product(parts, high, low):
-    return mm(parts[0], high) + (mm(parts[1], high) + mm(parts[0], low))
+def left_product(high, low, value):
+    a, b = parts_of(value)
+    n = value.shape[1]
+    wide = mm(high, jnp.concatenate([a, b], axis=1))
+    return wide[:, :n] + (wide[:, n:] + mm(low, a))
+
+
+def right_product(value, wide_table, high):
+    a, b = parts_of(value)
+    n = value.shape[1]
+    wide = mm(a, wide_table)
+    return wide[:, :n] + (wide[:, n:] + mm(b, high))
 
 
 def exact(a, b, ca, cb):
@@ -122,14 +133,19 @@
     rows = nx * ny
     crows = ncoarse // LANES
     halves = rows // LANES
-    (ls, vel, src, xrow) = refs[:4]
-    (lxh, lxl, lth, ltl, rzh, rzl, rth, rtl, sqh, sql, szh, szl) = refs[4:16]
-    mass = refs[16]
-    lev_out, p_out = refs[17:19]
+    given = refs[:15]
+    lev_hbm, p_hbm = refs[15:17]
+    held = refs[17:32]
+    (ls, vel, src, xrow, lxh, lxl, lth, ltl, rzb, rzh, rtb, rth, sqb, szb, mass) = held
     (
         qs, ysend, zsend, recvf, recvz, az, msg, arp, arz, xnb, xin, zmask, phi, wt, ibw, scaled, invd,
         rf, zf, pf, apf, mv, ends, sxy, rxy, rzs, ssa, rpa, rza, xss, xrs,
-    ) = refs[19:]
+        arps, arzs, phit, lsem, lev_out, p_out, osem,
+    ) = refs[32:]
+
+    loads = [pltpu.make_async_copy(a, b, lsem.at[n]) for n, (a, b) in enumerate(zip(given, held))]
+    for n in (3, 14, 0, 4, 5, 8, 9, 1, 2, 6, 7, 10, 11, 12, 13):
+        loads[n].start()
 
     me = [lax.axis_index(a) for a in AXES]
 
@@ -141,6 +157,22 @@
 
     plane_peers = [(i, j, 0) for i in range(sx) for j in range(sy) if (i, j) != (0, 0)]
     line_peers = [(0, 0, k) for k in range(1, sz)]
+
+    def distance(o):
+        return sum(min(o[i] % sizes[i], -o[i] % sizes[i]) * (1 if i else 0.5) for i in range(3))
+
+    plane_peers.sort(key=distance, reverse=True)
+    line_peers.sort(key=distance, reverse=True)
+    around = sorted(OFFSETS, key=lambda o: -sum(map(abs, o)))
+
+    barrier = pltpu.get_barrier_semaphore()
+    peers = sorted(
+        {tuple(o[i] % sizes[i] for i in range(3)) for o in OFFSETS}
+        | set(plane_peers)
+        | set(line_peers)
+    )
+    for o in peers:
+        pl.semaphore_signal(barrier, inc=1, device_id=device(o), device_id_type=MESH)
 
     has_lo = [jnp.where(me[i] > 0, 1.0, 0.0).astype(jnp.float32) for i in range(3)]
     has_hi = [jnp.where(me[i] < sizes[i] - 1, 1.0, 0.0).astype(jnp.float32) for i in range(3)]
@@ -159,6 +191,7 @@
 
     weight = inverse_copies(row_x, nx, 0) * inverse_copies(row_y, ny, 1) * inverse_copies(lane, nz, 2)
     wt[...] = weight
+    loads[14].wait()
     ibw[...] = weight / mass[...]
 
     def spread_shape(index, extent, dim, which):
@@ -179,6 +212,11 @@
     k9, kx, ky = split_nine(16)
     both = spread_shape(flat_x, nx, 0, kx) * spread_shape(flat_y, ny, 1, ky)
     phi[...] = jnp.where(k9 < 9, both, 0.0)
+    k48 = lax.broadcasted_iota(jnp.int32, (1, 48), 1)
+    k48 = lax.bitwise_and(k48, 15)
+    first = jnp.where(k48 >= 3, 1, 0) + jnp.where(k48 >= 6, 1, 0)
+    both = spread_shape(row_x, nx, 0, first) * spread_shape(row_y, ny, 1, k48 - 3 * first)
+    phit[...] = jnp.where(k48 < 9, both, 0.0).astype(jnp.bfloat16)
     phi_z = [spread_shape(lane, nz, 2, jnp.full((1, nz), kz, jnp.int32)) for kz in range(3)]
 
     k18 = lax.broadcasted_iota(jnp.int32, (18, 1), 0)
@@ -197,13 +235,8 @@
     wide_lane = lax.broadcasted_iota(jnp.int32, (18, nz), 1)
     target = jnp.where(k18 < 9, 0, nz - 1)
     ends[...] = jnp.where(wide_lane == target, 1.0, 0.0)
-    pick_row = lax.broadcasted_iota(jnp.int32, (8, nz), 0)
-    pick_lane = lax.broadcasted_iota(jnp.int32, (8, nz), 1)
-    pick = jnp.where(
-        ((pick_row == 0) & (pick_lane == 0)) | ((pick_row == 1) & (pick_lane == nz - 1)), 1.0, 0.0
-    )
-
     xnb[...] = jnp.zeros_like(xnb)
+    loads[3].wait()
     for j in range(crows):
         xnb[1, 4:5, j * LANES : (j + 1) * LANES] = xrow[j : j + 1, :]
     for par in range(2):
@@ -212,16 +245,6 @@
     apf[...] = jnp.zeros_like(apf)
     mv[...] = jnp.zeros_like(mv)
     p_out[...] = jnp.zeros_like(p_out)
-
-    barrier = pltpu.get_barrier_semaphore()
-    peers = sorted(
-        {tuple(o[i] % sizes[i] for i in range(3)) for o in OFFSETS}
-        | set(plane_peers)
-        | set(line_peers)
-    )
-    for o in peers:
-        pl.semaphore_signal(barrier, inc=1, device_id=device(o), device_id_type=MESH)
-    pl.semaphore_wait(barrier, len(peers))
 
     def remote(source, dest, send, recv, offset):
         return pltpu.make_async_remote_copy(
@@ -239,13 +262,9 @@
     def nine(o):
         return (1 - o[0]) * 3 + (1 - o[1])
 
-    for o in OFFSETS:
-        place = pl.ds(OFFSETS.index(o) * crows, crows)
-        remote(xrow, xin.at[place, :], xss.at[0], xrs.at[0], o).start()
-
     face_rows = 2 * ny + 2 * nx
 
-    def halo_start(value, slot):
+    def halo_pack(value, slot):
         inside = lax.bitwise_and(lane, NP - 1)
         up = (inside == NP - 1) & (lane < nz - 1)
         down = (inside == 0) & (lane > 0)
@@ -266,7 +285,8 @@
             field[e * ny : (e + 1) * ny, :] = total
         ysend[slot, 0] = field[pl.ds(0, nx, stride=ny), :]
         ysend[slot, 1] = field[pl.ds(ny - 1, nx, stride=ny), :]
-        face = exact(pick, field[...], 1, 1)
+        across = jnp.transpose(field[...])
+        face = jnp.concatenate([across[0:1], across[nz - 1 : nz]], axis=0)
         for dx in (-1, 0, 1):
             for dy in (-1, 0, 1):
                 shift = (-ny * dx + (ny - 1) * dy) % rows
@@ -276,8 +296,10 @@
                     part = moved[0:2, h * LANES : (h + 1) * LANES]
                     zsend[slot, place, h : h + 1, :] = part[0:1]
                     zsend[slot, place, halves + h : halves + h + 1, :] = part[1:2]
+
+    def halo_send(slot):
         send, recv = sxy.at[slot], rxy.at[slot]
-        for o in OFFSETS:
+        for o in around:
             if o[2] != 0:
                 k, hi = nine(o), 1 if o[2] > 0 else 0
                 remote(
@@ -287,7 +309,7 @@
                     rzs.at[slot, 1],
                     o,
                 ).start()
-        for o in OFFSETS:
+        for o in around:
             if o[2] == 0:
                 x_row = 0 if o[0] < 0 else (nx - 1) * ny
                 y_row = 0 if o[1] < 0 else ny - 1
@@ -302,6 +324,10 @@
                     place = face_rows + (0 if o[0] > 0 else 2) + (0 if o[1] > 0 else 1)
                     count = 1
                 remote(source, recvf.at[slot, pl.ds(place, count), :], send, recv, o).start()
+
+    def halo_start(value, slot):
+        halo_pack(value, slot)
+        halo_send(slot)
 
     def halo_finish(slot):
         drain(recvf.at[slot], rxy.at[slot])
@@ -335,6 +361,22 @@
                 msg.at[par, 0, pl.ds(0, mrows), :], arp.at[par, n], ssa.at[par, 0], rpa.at[par], o
             ).start()
 
+    def sum_of_row():
+        own = pl.ds(crows, 1)
+        for n, o in enumerate(plane_peers):
+            place = arps.at[pl.ds(n, 1), :]
+            remote(msg.at[1, 0, own, :], place, ssa.at[2, 0], rpa.at[2], o).start()
+        drain(arps, rpa.at[2])
+        here = msg[1, 0, crows : crows + 1] + jnp.sum(arps[...], axis=0, keepdims=True)
+        msg[1, 1, crows : crows + 1] = here
+        for n, o in enumerate(line_peers):
+            place = arzs.at[pl.ds(n, 1), :]
+            remote(msg.at[1, 1, own, :], place, ssa.at[2, 1], rza.at[2], o).start()
+        drain(arzs, rza.at[2])
+        drain(arps, ssa.at[2, 0])
+        drain(arzs, ssa.at[2, 1])
+        return here + jnp.sum(arzs[...], axis=0, keepdims=True)
+
     def plane_finish_line_start(par):
         drain(arp.at[par], rpa.at[par])
         msg[par, 1, 0:mrows] = msg[par, 0, 0:mrows] + jnp.sum(arp[par], axis=0)
@@ -351,14 +393,11 @@
         return total
 
     def grad(value):
-        parts = parts_of(value)
-        gxy = left_product(lxh[...], lxl[...], parts)
-        return gxy, right_product(parts, rzh[...], rzl[...])
+        gxy = left_product(lxh[...], lxl[...], value)
+        return gxy, right_product(value, rzb[...], rzh[...])
 
     def grad_transposed(wxy, wz):
-        return left_product(lth[...], ltl[...], parts_of(wxy)) + right_product(
-            parts_of(wz), rth[...], rtl[...]
-        )
+        return left_product(lth[...], ltl[...], wxy) + right_product(wz, rtb[...], rth[...])
 
     def twice(value):
         return jnp.concatenate([value, value], axis=0)
@@ -373,25 +412,31 @@
             for j in range(1, crows):
                 product = product + xnb[kz, :, j * LANES : (j + 1) * LANES] * coarse[j : j + 1, :]
             acc = acc + jnp.sum(product, axis=1, keepdims=True) * phi_z[kz]
-        return exact(phi[...], acc, 0, 0)
-
+        high, low = parts_of(acc)
+        rest = (acc - high.astype(jnp.float32) - low.astype(jnp.float32)).astype(jnp.bfloat16)
+        return mm(phit[...], jnp.concatenate([high, low, rest], axis=0))
+
+    for n in (0, 4, 5, 8, 9, 1):
+        loads[n].wait()
     level = ls[...]
     gxy, gz = grad(level)
     advect = vel[0] * gxy[0:rows] + vel[1] * gxy[rows:] + vel[2] * gz
     b = mass[...]
-    halo_start(b * advect, 0)
-    halo_start(
+    halo_pack(b * advect, 0)
+    for n in (2, 6, 7, 10, 11):
+        loads[n].wait()
+    halo_pack(
         grad_transposed(jnp.concatenate([b * vel[0], b * vel[1]], axis=0), b * vel[2])
         + b * src[...],
         1,
     )
+    pl.semaphore_wait(barrier, len(peers))
+    halo_send(0)
+    halo_send(1)
+    for o in OFFSETS:
+        place = pl.ds(OFFSETS.index(o) * crows, crows)
+        remote(xrow, xin.at[place, :], xss.at[0], xrs.at[0], o).start()
     level = level - TIME_STEP * halo_finish(0) * ibw[...]
-    rhs = SOURCE_SCALE * halo_finish(1)
-    rf[...] = rhs
-    restricted = total_of(wt[...] * rhs)
-    for j in range(crows):
-        msg[1, 0, j : j + 1, :] = restricted * xrow[j : j + 1, :]
-    plane_start(1)
     for sweep in range(RSWEEPS):
         gxy, gz = grad(level)
         gx, gy = gxy[0:rows], gxy[rows:]
@@ -400,16 +445,26 @@
         slot = (2 + sweep) % 3
         halo_start(grad_transposed(twice(factor) * gxy, factor * gz), slot)
         if sweep == 0:
+            rhs = SOURCE_SCALE * halo_finish(1)
+            rf[...] = rhs
+            restricted = total_of(wt[...] * rhs)
+            for j in range(crows):
+                msg[1, 0, j : j + 1, :] = restricted * xrow[j : j + 1, :]
+            plane_start(1)
+        else:
             plane_finish_line_start(1)
         level = level + PSEUDO_STEP * halo_finish(slot) * ibw[...]
     lev_out[...] = level
+    level_copy = pltpu.make_async_copy(lev_out, lev_hbm, osem.at[0])
+    level_copy.start()
 
     b = mass[...]
     sc = b / (GAS_DENSITY + (1.0 - GAS_DENSITY) * jnp.clip(level, 0.0, 1.0))
     scaled[...] = sc
-    parts = parts_of(sc)
+    for n in (12, 13):
+        loads[n].wait()
     halo_start(
-        left_product(sqh[...], sql[...], parts) + right_product(parts, szh[...], szl[...]) + b, 1
+        left_product(sqb[0], sqb[1], sc) + right_product(sc, szb[...], szb[:, 0:nz]) + b, 1
     )
     coarse = line_finish(1)
     mv[0, 0:crows] = coarse[0:crows]
@@ -440,8 +495,7 @@
             lane1 == 0, inner, jnp.where(lane1 == 1, energy, jnp.where(lane1 == 2, cross, 0.0))
         )
 
-    def steps_from(total, step):
-        sums = total[crows : crows + 1, :]
+    def steps_from(sums, step):
         inner, energy, cross = sums[:, 0:1], sums[:, 1:2], sums[:, 2:3]
         old_inner, old_curve = mv[2, 0:1, 0:1], mv[2, 1:2, 0:1]
         ratio = jnp.where(step > 0, inner / old_inner, 0.0)
@@ -454,7 +508,9 @@
         slot = lax.rem(step, 2)
         z = zf[...]
         q = element_operator(z)
-        tested = exact(phi[...], q, 1, 0)
+        high, low = parts_of(q)
+        wide = mm(phi[...].astype(jnp.bfloat16), jnp.concatenate([high, low], axis=1))
+        tested = wide[:, :nz] + wide[:, nz:]
         columns = [jnp.sum(tested * phi_z[kz], axis=1, keepdims=True) for kz in range(3)]
         for j in range(crows):
             part = columns[0] * xnb[0, :, j * LANES : (j + 1) * LANES]
@@ -467,7 +523,7 @@
         plane_finish_line_start(slot)
         az_now = halo_finish(slot)
         total = line_finish(slot)
-        inner, ratio, curve, size = steps_from(total, step)
+        inner, ratio, curve, size = steps_from(total[crows : crows + 1, :], step)
         p = z + ratio * pf[...]
         ap = az_now + ratio * apf[...]
         pf[...] = p
@@ -485,13 +541,14 @@
 
     lax.fori_loop(0, ITERS - 1, iteration, 0)
 
-    par = (ITERS - 1) % 2
     z = zf[...]
-    send_sums(par, z, element_operator(z))
-    plane_start(par)
-    plane_finish_line_start(par)
-    _, ratio, _, size = steps_from(line_finish(par), ITERS - 1)
+    send_sums(1, z, element_operator(z))
+    _, ratio, _, size = steps_from(sum_of_row(), ITERS - 1)
     p_out[...] += size * (z + ratio * pf[...])
+    pressure_copy = pltpu.make_async_copy(p_out, p_hbm, osem.at[1])
+    pressure_copy.start()
+    level_copy.wait()
+    pressure_copy.wait()
 
 
 def body(sizes, level_set, velocity, source, coarse_factor):
@@ -499,7 +556,7 @@
     rows = nx * ny
     ncoarse = coarse_factor.shape[1]
     crows = ncoarse // LANES
-    tables, mass = block_tables(nx, ny, nz)
+    tables = block_tables(nx, ny, nz)
     sx, sy, sz = sizes
     f32 = jnp.float32
 
@@ -509,7 +566,14 @@
     dma = pltpu.SemaphoreType.DMA
     face_rows = 2 * ny + 2 * nx
     halves = rows // LANES
-    scratch = [
+    operands = [
+        level_set.reshape(rows, nz),
+        velocity.reshape(3, rows, nz),
+        source.reshape(rows, nz),
+        coarse_factor.reshape(crows, LANES),
+        *[jnp.asarray(t) for t in tables],
+    ]
+    scratch = [pltpu.VMEM(a.shape, a.dtype) for a in operands] + [
         vm(3, rows, nz),
         vm(3, 2, nx, nz),
         vm(3, 9, 2 * halves, LANES),
@@ -536,31 +600,30 @@
         dma((3,)),
         dma((3,)),
         dma((3, 2)),
-        dma((2, 2)),
-        dma((2,)),
-        dma((2,)),
+        dma((3, 2)),
+        dma((3,)),
+        dma((3,)),
         dma((1,)),
         dma((1,)),
+        vm(sx * sy - 1, LANES),
+        vm(sz - 1, LANES),
+        pltpu.VMEM((rows, 48), jnp.bfloat16),
+        dma((len(operands),)),
+        vm(rows, nz),
+        vm(rows, nz),
+        dma((2,)),
     ]
-    flat = level_set.reshape(rows, nz)
     level, pressure = pl.pallas_call(
         functools.partial(kernel, (sizes, nx, ny, nz, ncoarse)),
         out_shape=(jax.ShapeDtypeStruct((rows, nz), f32),) * 2,
-        in_specs=[pl.BlockSpec(memory_space=pltpu.VMEM)] * (5 + len(tables)),
-        out_specs=(pl.BlockSpec(memory_space=pltpu.VMEM),) * 2,
+        in_specs=[pl.BlockSpec(memory_space=pltpu.HBM)] * len(operands),
+        out_specs=(pl.BlockSpec(memory_space=pltpu.HBM),) * 2,
         scratch_shapes=scratch,
         compiler_params=pltpu.CompilerParams(
-            collective_id=0, has_side_effects=True, vmem_limit_bytes=48 * 1024 * 1024
+            collective_id=0, has_side_effects=True, vmem_limit_bytes=63 * 1024 * 1024
         ),
         name="transport_and_pressure",
-    )(
-        flat,
-        velocity.reshape(3, rows, nz),
-        source.reshape(rows, nz),
-        coarse_factor.reshape(crows, LANES),
-        *[jnp.asarray(t) for t in tables],
-        jnp.asarray(mass),
-    )
+    )(*operands)
     return level.reshape(nx, ny, nz), pressure.reshape(nx, ny, nz)
 
 

time: 148 us -> 120 us (0.81)
  Pallas kernels: 131 us -> 117 us
  local copies, waits for them, and re-layouts: 15.8 us -> 2.26 us
    pallas_call x1, Pallas kernels: 131 us -> 117 us  [body(): pl.pallas_call(functools.partial(kernel, (sizes, nx, ny, nz, ncoarse)), o...]
    unnamed x36 -> x4, local copies, waits for them, and re-layouts: 15.8 us -> 2.26 us
where the time goes in v2:
time: 120 us
  Pallas kernels  117 us (98%)
  local copies, waits for them, and re-layouts  2.26 us (2%)
    pallas_call x1, Pallas kernels, body(): pl.pallas_call(functools.partial(kernel, (sizes, nx, ny, nz, ncoarse)), o...  117 us

profile of v2, /device:TPU:1, one launch (start us, length us, event | category | flops | bytes accessed | tf_op | source)
XLA Modules:
  0.0 120.1 jit_solution(6495870588399846544)
XLA Ops:
  0.6 117.2 %transport_and_pressure.1 = (f32[256,128]{1,0:T(8,128)}, f32[256,128]{1,0:T(8,128)}) custom-call(f32[256,128]{1,0:T(8,128)} %bitcast.9, f32[3,256,128]{2,1,0:T(8,128)} %bitcast.6, f32[256,128]{1,0:T(8,128)} %bitcast.10, f32[4,128]{1,0:T(4,128)} %bitcast.11, bf16[512,256]{1,0:T(8,128)(2,1)} %constant.22.clone.refs_4_, ...), custom_call_target="tpu_custom_call" | custom-call | tf_op jit(solution)/shard_map/transport_and_pressure/pallas_call | solution.py:616
  117.8 0.0 copy-start
  117.8 1.6 %copy.19 = f32[16,16,128]{2,1,0:T(8,128)} copy(f32[16,16,128]{2,1,0:T(8,128)} %bitcast.8) | data formatting | bytes 262144
  119.4 0.0 copy-done
  119.5 0.7 copy.20
Async XLA Ops:
  117.8 1.6 %copy-start = (f32[256,128]{1,0:T(8,128)S(1)}, f32[256,128]{1,0:T(8,128)}, u32[]{:S(2)}) copy-start(f32[256,128]{1,0:T(8,128)} %get-tuple-element.5) | copy-start | bytes 393220

commit v3 on v2

--- a/solution.py
+++ b/solution.py
@@ -121,12 +121,6 @@
     return wide[:, :n] + (wide[:, n:] + mm(b, high))
 
 
-def exact(a, b, ca, cb):
-    return lax.dot_general(
-        a, b, (((ca,), (cb,)), ((), ())), precision=HIGHEST, preferred_element_type=jnp.float32
-    )
-
-
 def kernel(cfg, *refs):
     sizes, nx, ny, nz, ncoarse = cfg
     sx, sy, sz = sizes
@@ -139,13 +133,11 @@
     (ls, vel, src, xrow, lxh, lxl, lth, ltl, rzb, rzh, rtb, rth, sqb, szb, mass) = held
     (
         qs, ysend, zsend, recvf, recvz, az, msg, arp, arz, xnb, xin, zmask, phi, wt, ibw, scaled, invd,
-        rf, zf, pf, apf, mv, ends, sxy, rxy, rzs, ssa, rpa, rza, xss, xrs,
+        rf, zf, pf, apf, mv, sxy, rxy, rzs, ssa, rpa, rza, xss, xrs,
         arps, arzs, phit, lsem, lev_out, p_out, osem,
     ) = refs[32:]
 
     loads = [pltpu.make_async_copy(a, b, lsem.at[n]) for n, (a, b) in enumerate(zip(given, held))]
-    for n in (3, 14, 0, 4, 5, 8, 9, 1, 2, 6, 7, 10, 11, 12, 13):
-        loads[n].start()
 
     me = [lax.axis_index(a) for a in AXES]
 
@@ -171,8 +163,11 @@
         | set(plane_peers)
         | set(line_peers)
     )
+    peers.sort(key=distance, reverse=True)
     for o in peers:
         pl.semaphore_signal(barrier, inc=1, device_id=device(o), device_id_type=MESH)
+    for n in (3, 14, 0, 4, 5, 8, 9, 1, 2, 6, 7, 10, 11, 12, 13):
+        loads[n].start()
 
     has_lo = [jnp.where(me[i] > 0, 1.0, 0.0).astype(jnp.float32) for i in range(3)]
     has_hi = [jnp.where(me[i] < sizes[i] - 1, 1.0, 0.0).astype(jnp.float32) for i in range(3)]
@@ -232,9 +227,6 @@
 
     side = jnp.where(upper == 0, has_lo[2], has_hi[2])
     zmask[...] = region(flat_x, nx, 0, zx) * region(flat_y, ny, 1, zy) * side
-    wide_lane = lax.broadcasted_iota(jnp.int32, (18, nz), 1)
-    target = jnp.where(k18 < 9, 0, nz - 1)
-    ends[...] = jnp.where(wide_lane == target, 1.0, 0.0)
     xnb[...] = jnp.zeros_like(xnb)
     loads[3].wait()
     for j in range(crows):
@@ -335,7 +327,12 @@
         for h in range(halves):
             piece = slice(h * LANES, (h + 1) * LANES)
             arrived = recvz[slot, pl.ds(h, 18, stride=halves), :] * zmask[:, piece]
-            az[piece, :] = qs[slot, piece, :] + exact(arrived, ends[...], 0, 0)
+            low = jnp.sum(arrived[0:9], axis=0, keepdims=True)
+            high = jnp.sum(arrived[9:18], axis=0, keepdims=True)
+            pair = jnp.concatenate([low, high, jnp.zeros((6, LANES), jnp.float32)], axis=0)
+            down = jnp.transpose(pair)
+            at_ends = jnp.where(lane == 0, down[:, 0:1], jnp.where(lane == nz - 1, down[:, 1:2], 0.0))
+            az[piece, :] = qs[slot, piece, :] + at_ends
         faces = recvf.at[slot]
         az[0:ny, :] += faces[0:ny, :] * has_lo[0]
         az[rows - ny : rows, :] += faces[ny : 2 * ny, :] * has_hi[0]
@@ -521,19 +518,20 @@
         plane_start(slot)
         halo_start(q, slot)
         plane_finish_line_start(slot)
+        p_out[...] += mv[2, 2:3, 0:1] * pf[...]
         az_now = halo_finish(slot)
         total = line_finish(slot)
         inner, ratio, curve, size = steps_from(total[crows : crows + 1, :], step)
-        p = z + ratio * pf[...]
+        coarse_step = total[0:crows] + ratio * mv[1, 0:crows]
+        coarse = mv[0, 0:crows] - size * coarse_step
+        mv[1, 0:crows] = coarse_step
+        mv[0, 0:crows] = coarse
         ap = az_now + ratio * apf[...]
-        pf[...] = p
+        r = rf[...] - size * ap
         apf[...] = ap
-        p_out[...] += size * p
-        r = rf[...] - size * ap
         rf[...] = r
-        mv[1, 0:crows] = total[0:crows] + ratio * mv[1, 0:crows]
-        coarse = mv[0, 0:crows] - size * mv[1, 0:crows]
-        mv[0, 0:crows] = coarse
+        pf[...] = z + ratio * pf[...]
+        mv[2, 2:3, :] = jnp.broadcast_to(size, (1, LANES))
         mv[2, 0:1, :] = jnp.broadcast_to(inner, (1, LANES))
         mv[2, 1:2, :] = jnp.broadcast_to(curve, (1, LANES))
         zf[...] = r * invd[...] + spread(coarse)
@@ -544,7 +542,7 @@
     z = zf[...]
     send_sums(1, z, element_operator(z))
     _, ratio, _, size = steps_from(sum_of_row(), ITERS - 1)
-    p_out[...] += size * (z + ratio * pf[...])
+    p_out[...] = (p_out[...] + mv[2, 2:3, 0:1] * pf[...]) + size * (z + ratio * pf[...])
     pressure_copy = pltpu.make_async_copy(p_out, p_hbm, osem.at[1])
     pressure_copy.start()
     level_copy.wait()
@@ -596,7 +594,6 @@
         vm(rows, nz),
         vm(rows, nz),
         vm(3, 8, LANES),
-        vm(18, nz),
         dma((3,)),
         dma((3,)),
         dma((3, 2)),

time: 120 us -> 120 us (level)
  no operation moved by 1% of the time
where the time goes in v3:
time: 120 us
  Pallas kernels  117 us (98%)
  local copies, waits for them, and re-layouts  2.26 us (2%)
    pallas_call x1, Pallas kernels, body(): pl.pallas_call(functools.partial(kernel, (sizes, nx, ny, nz, ncoarse)), o...  117 us

profile of v3, /device:TPU:1, one launch (start us, length us, event | category | flops | bytes accessed | tf_op | source)
XLA Modules:
  0.0 119.6 jit_solution(4648511193814674048)
XLA Ops:
  0.6 116.7 %transport_and_pressure.1 = (f32[256,128]{1,0:T(8,128)}, f32[256,128]{1,0:T(8,128)}) custom-call(f32[256,128]{1,0:T(8,128)} %bitcast.9, f32[3,256,128]{2,1,0:T(8,128)} %bitcast.6, f32[256,128]{1,0:T(8,128)} %bitcast.10, f32[4,128]{1,0:T(4,128)} %bitcast.11, bf16[512,256]{1,0:T(8,128)(2,1)} %constant.22.clone.refs_4_, ...), custom_call_target="tpu_custom_call" | custom-call | tf_op jit(solution)/shard_map/transport_and_pressure/pallas_call | solution.py:613
  117.4 0.0 copy-start
  117.4 1.6 %copy.19 = f32[16,16,128]{2,1,0:T(8,128)} copy(f32[16,16,128]{2,1,0:T(8,128)} %bitcast.8) | data formatting | bytes 262144
  119.0 0.0 copy-done
  119.0 0.7 copy.20
Async XLA Ops:
  117.4 1.6 %copy-start = (f32[256,128]{1,0:T(8,128)S(1)}, f32[256,128]{1,0:T(8,128)}, u32[]{:S(2)}) copy-start(f32[256,128]{1,0:T(8,128)} %get-tuple-element.5) | copy-start | bytes 393220
